TPU v7x, 32 devices: a whole 2x2x4 slice. The times are simulated.
32 devices in a mesh: abl: 2 (over y), head: 4 (over x, core), ctx: 4 (over z).
Axes of the slice: x: 2, y: 2, z: 4, core: 2. Of those that a mesh axis runs over, the one named last changes fastest.
Arguments:
- queries: bfloat16 [1024, 6144], P(('abl', 'head', 'ctx')), parts along dimension 0, may hold values from -30 to 30
- keys: bfloat16 [16384, 6144], P(('abl', 'ctx'), 'head'), parts along dimension 0, may hold values from -6 to 6
- values: bfloat16 [16384, 6144], P(('abl', 'ctx'), 'head'), parts along dimension 0, may hold values from -6 to 6
- kept_rows: int32 [128], P(('abl', 'ctx')), parts along dimension 0, may hold values from 0 to 1, as said below
- out_weight: bfloat16 [6144, 6144], P('head'), may hold values from -6 to 6
Outputs:
- projected: bfloat16 [1024, 6144], P(('abl', 'head', 'ctx')), parts along dimension 0
There are 2 independent parts, one for each index of `abl`. A program takes and returns all parts, laid end to end along the dimension named above; an argument that names none is the same for every part. Nothing has to cross between parts.
Inputs may be any that keep to these rules, and one draw needn't show every extreme that they name: `kept_rows`: in every part the first row of each block of 16 consecutive rows is kept.
All inputs are finite; a program needn't handle non-finite values.
Results may differ from a plain program's by a relative error of at most 0.028.
Values may be sent and summed in bfloat16 or wider, within the bound.
No kernel may reach another device: no remote copies, remote signals or barrier semaphores. Data moves between devices by JAX's collectives and lax.ppermute only.
A program may use at most 128 MiB of HBM per device.

v0:
```python
import math
import jax
import jax.numpy as jnp
from jax import lax
from jax.sharding import PartitionSpec as P

HD = 128


def shards(queries, keys, values, kept_rows, out_weight):
    score_scale = 1.0 / math.sqrt(HD)
    local_heads = keys.shape[1] // HD
    key_count = keys.shape[0]
    key_heads = keys.reshape(key_count, local_heads, HD)
    value_heads = values.reshape(key_count, local_heads, HD)
    visible = jnp.repeat(kept_rows, 128) > 0
    query_block = lax.all_to_all(queries, "head", split_axis=1, concat_axis=0, tiled=True)
    all_queries = lax.all_gather(query_block, "ctx", axis=0, tiled=True)
    row_count = all_queries.shape[0]
    zeros_sum = jnp.zeros((row_count, local_heads * HD), jnp.float32)
    lowest = jnp.full((local_heads, row_count), -1e30, jnp.float32)
    summed = zeros_sum
    row_count = all_queries.shape[0]
    shaped = all_queries.reshape(row_count, local_heads, HD)
    scores = (
        jnp.einsum("qhd,khd->hqk", shaped, key_heads, preferred_element_type=jnp.float32)
        * score_scale
    )
    scores = jnp.where(visible[None, None, :], scores, -jnp.inf)
    highest = jnp.maximum(lowest, jnp.max(scores, axis=-1))
    rescale = jnp.exp(lowest - highest)
    softened = jnp.exp(scores - highest[..., None])
    normal_sum = jnp.sum(softened, axis=-1)
    mixed = jnp.einsum(
        "hqk,khd->qhd",
        softened.astype(jnp.bfloat16),
        value_heads,
        preferred_element_type=jnp.float32,
    )
    summed = summed * jnp.repeat(rescale.T, HD, axis=1) + mixed.reshape(row_count, local_heads * HD)
    summed, running, normal_sum = (summed, highest, normal_sum)
    highest = lax.pmax(running, "ctx")
    rescale = jnp.exp(running - highest)
    summed = summed * jnp.repeat(rescale.T, HD, axis=1)
    normal_sum = normal_sum * rescale
    summed, normal_sum = (
        lax.psum_scatter(
            summed.astype(jnp.bfloat16), "ctx", scatter_dimension=0, tiled=True
        ).astype(jnp.float32),
        lax.psum_scatter(
            normal_sum.astype(jnp.bfloat16), "ctx", scatter_dimension=1, tiled=True
        ).astype(jnp.float32),
    )
    attended = (summed / jnp.repeat(normal_sum.T, HD, axis=1)).astype(jnp.bfloat16)
    return lax.psum_scatter(
        jnp.dot(attended, out_weight, preferred_element_type=jnp.float32).astype(jnp.bfloat16),
        "head",
        scatter_dimension=0,
        tiled=True,
    )


def solution(mesh):
    placed = (
        P(("abl", "head", "ctx"), None),
        P(("abl", "ctx"), "head"),
        P(("abl", "ctx"), "head"),
        P(("abl", "ctx")),
        P("head", None),
    )
    return jax.shard_map(
        shards,
        mesh=mesh,
        in_specs=placed,
        out_specs=P(("abl", "head", "ctx"), None),
        check_vma=False,
    )
```

profile of v0, /device:TPU:0, one launch (start us, length us, event | category | flops | bytes accessed | tf_op | source)
XLA Modules:
  0.0 223.1 jit_solution(14071060724346164999)
XLA Ops:
  6.5 1.0 copy.33
  7.6 11.6 %all_to_all.19 = bf16[32,4,1536]{2,0,1:T(8,128)(2,1)} all-to-all(bf16[32,4,1536]{2,0,1:T(8,128)(2,1)S(1)} %bitcast.42), channel_id=1, replica_groups=mesh['abl'=2,'head'=4,'ctx'=4] {'head'}, dimensions={1} | all-to-all | bytes 786432 | tf_op jit(solution)/shard_map/all_to_all | solution.py:17
  19.1 0.0 all-gather.2.cloned.1.call-update
  19.2 0.0 reduce-scatter.12.cloned.1.call-start
  19.2 8.8 %copy.21 = bf16[2048,1536]{0,1:T(8,128)(2,1)} copy(bf16[2048,1536]{1,0:T(8,128)(2,1)} %param.6) | data formatting | bytes 12582912 | tf_op args[1]
  28.0 8.8 %copy.24 = bf16[2048,1536]{0,1:T(8,128)(2,1)} copy(bf16[2048,1536]{1,0:T(8,128)(2,1)} %param.7) | data formatting | bytes 12582912 | tf_op args[2]
  36.7 0.1 broadcast_bitcast_fusion
  36.8 20.3 %all-gather.2.cloned.1.call-done = bf16[512,1536]{1,0:T(8,128)(2,1)} async-done(((bf16[128,1536]{1,0:T(8,128)(2,1)}), bf16[512,1536]{1,0:T(8,128)(2,1)}) %all-gather.2.cloned.1.call-update) | async-done | bytes 1572880 | tf_op jit(solution)/shard_map/all_gather | solution.py:18
  57.1 1.7 copy.20
  58.8 22.6 %fusion = (f32[12,512]{1,0:T(8,128)S(1)}, f32[12,512,2048]{2,1,0:T(8,128)}) fusion(pred[2048]{0:T(1024)(128)(4,1)S(1)} %broadcast_bitcast_fusion, bf16[512,12,128]{0,2,1:T(8,128)(2,1)S(1)} %bitcast.38, bf16[2048,12,128]{0,2,1:T(8,128)(2,1)} %bitcast.37), kind=kOutput, calls=%fused_computation.2 | convolution fusion | flops 3258968064 | bytes 58222592 | tf_op jit(solution)/shard_map/qhd,khd->hqk/dot_general | solution.py:26
  81.4 16.9 %pmax.7 = f32[12,512]{1,0:T(8,128)S(1)} all-reduce(f32[12,512]{1,0:T(8,128)S(1)} %broadcast_maximum_fusion), channel_id=1, replica_groups=mesh['abl'=2,'head'=4,'ctx'=4] {'ctx'}, use_global_device_ids=true, to_apply=%region_1.2 | all-reduce | flops 6144 | bytes 49152 | tf_op jit(solution)/shard_map/pmax | solution.py:42
  98.4 21.1 %fusion.1 = f32[12,512]{1,0:T(8,128)S(1)} fusion(f32[12,512,2048]{2,1,0:T(8,128)} %get-tuple-element.9, f32[12,512]{1,0:T(8,128)S(1)} %broadcast_maximum_fusion, pred[2048]{0:T(1024)(128)(4,1)S(1)} %broadcast_bitcast_fusion), kind=kLoop, calls=%fused_computation.3 | loop fusion | flops 50325504 | bytes 50382848 | tf_op jit(solution)/shard_map/reduce_sum | solution.py:33
  119.5 0.8 copy.29
  120.3 0.0 reduce-scatter.10.cloned.1.call-start
  120.4 22.0 %fusion.7 = bf16[512,12,128]{0,2,1:T(8,128)(2,1)S(1)} fusion(bf16[2048,12,128]{0,2,1:T(8,128)(2,1)} %bitcast.39, f32[12,512,2048]{2,1,0:T(8,128)} %get-tuple-element.9, f32[12,512]{1,0:T(8,128)S(1)} %broadcast_maximum_fusion, pred[2048]{0:T(1024)(128)(4,1)S(1)} %broadcast_bitcast_fusion, f32[512,12]{0,1:T(8,128)S(1)} %get-tuple-element.6, ...), kind=kOutput, calls=%fused_computation.10 | convolution fusion | flops 3273916416 | bytes 58271744 | tf_op jit(solution)/shard_map/hqk,khd->qhd/dot_general | solution.py:34
  142.4 1.6 copy.27
  144.0 0.2 reduce-scatter.8.cloned.1.call-start
  144.2 0.0 reduce-scatter.12.cloned.1.call-done
  144.3 0.8 copy.30
  145.1 32.7 %reduce-scatter.10.cloned.1.call-done = bf16[128,1536]{1,0:T(8,128)(2,1)} async-done(((bf16[512,1536]{1,0:T(8,128)(2,1)}), bf16[128,1536]{1,0:T(8,128)(2,1)}) %reduce-scatter.10.cloned.1.call-update) | async-done | bytes 393232
  177.7 1.2 copy.28
  179.0 0.1 fusion.10
  179.1 10.2 %convolution_convert_fusion = bf16[128,6144]{1,0:T(8,128)(2,1)} fusion(bf16[128,1536]{0,1:T(8,128)(2,1)S(1)} %fusion.10, bf16[1536,6144]{1,0:T(8,128)(2,1)} %param.9), kind=kOutput, calls=%fused_computation.7 | convolution fusion | flops 2416705536 | bytes 20840448 | tf_op jit(solution)/shard_map/dot_general | solution.py:56
  189.3 27.3 %reduce-scatter.8.cloned.1.call-done = bf16[32,6144]{1,0:T(8,128)(2,1)} async-done(((bf16[128,6144]{1,0:T(8,128)(2,1)}), bf16[32,6144]{1,0:T(8,128)(2,1)}) %reduce-scatter.8.cloned.1.call-update) | async-done | bytes 393232 | tf_op jit(solution)/shard_map/reduce_scatter | solution.py:55
  (10 shorter events, 0.1 us)
Async XLA Ops:
  6.5 30.2 %copy-start = (s32[16]{0:T(128)S(1)}, s32[16]{0:T(128)}, u32[]{:S(2)}) copy-start(s32[16]{0:T(128)} %param.8) | copy-start | bytes 196
  6.5 50.6 %all-gather.2.cloned.1.call-start = ((), (), s32[]{:S(2)}) async-start(), calls=%async_computation.4 | async-start | bytes 1966080 | tf_op jit(solution)/shard_map/all_gather | solution.py:18
  19.2 125.1 %reduce-scatter.12.cloned.1.call-start = ((), (), s32[]{:S(2)}) async-start(), calls=%async_computation.7 | async-start | bytes 163840
  120.3 57.4 %reduce-scatter.10.cloned.1.call-start = ((), (), s32[]{:S(2)}) async-start(), calls=%async_computation.6 | async-start | bytes 1966080
  144.0 72.6 %reduce-scatter.8.cloned.1.call-start = ((), (), s32[]{:S(2)}) async-start(), calls=%async_computation.5 | async-start | bytes 1966080 | tf_op jit(solution)/shard_map/reduce_scatter | solution.py:55
Sparse Core Ops, SparseCore 0:
  19.3 37.8 all-gather.1
  120.4 17.4 reduce-scatter.11
  144.1 33.5 reduce-scatter.9
  189.4 27.1 reduce-scatter.7
where the time goes:
time: 224 us; the launch traced here: 223 us
  waiting for transfers between devices  80.4 us (36%)
  matrix products  54.9 us (25%)
  blocking collectives  28.5 us (13%)
  local copies, waits for them, and re-layouts  24.7 us (11%)
  other arithmetic  21.2 us (9%)
  between operations  13.2 us (6%)
    unnamed x6, waiting for transfers between devices  32.7 us
    reduce_scatter x1, waiting for transfers between devices, shards(): lax.psum_scatter(jnp.dot(attended, out_weight, preferred_element_type=jnp...  27.3 us
    dot_general x1, matrix products, shards(): jnp.einsum('qhd,khd->hqk', shaped, key_heads, preferred_element_type=jnp....  22.6 us
    dot_general x1, matrix products, shards(): jnp.einsum('hqk,khd->qhd', softened.astype(jnp.bfloat16), value_heads, pr...  22 us
    unnamed x8, local copies, waits for them, and re-layouts  21.9 us
    reduce_sum x1, other arithmetic, shards(): normal_sum = jnp.sum(softened, axis=-1)  21.1 us
    all_gather x1, waiting for transfers between devices, shards(): all_queries = lax.all_gather(query_block, 'ctx', axis=0, tiled=True)  20.3 us
    pmax x1, blocking collectives, shards(): highest = lax.pmax(running, 'ctx')  16.9 us
  transfers between devices with their start and end apart: 4, of which 3 were waited for; matrix products, arithmetic and copies ran while one was open for 19% of the time, Pallas kernels for 0%

commit v1 on v0

--- a/solution.py
+++ b/solution.py
@@ -3,6 +3,7 @@
 import jax.numpy as jnp
 from jax import lax
 from jax.sharding import PartitionSpec as P
+from jax.lax import all_to_all, axis_size
 
 HD = 128
 
@@ -14,7 +15,15 @@
     key_heads = keys.reshape(key_count, local_heads, HD)
     value_heads = values.reshape(key_count, local_heads, HD)
     visible = jnp.repeat(kept_rows, 128) > 0
-    query_block = lax.all_to_all(queries, "head", split_axis=1, concat_axis=0, tiled=True)
+    query_block = jnp.concatenate(
+        all_to_all(
+            jnp.stack(jnp.split(queries, axis_size("head"), axis=1), axis=0),
+            axis_name="head",
+            split_axis=0,
+            concat_axis=0,
+        ),
+        axis=0,
+    )
     all_queries = lax.all_gather(query_block, "ctx", axis=0, tiled=True)
     row_count = all_queries.shape[0]
     zeros_sum = jnp.zeros((row_count, local_heads * HD), jnp.float32)

time: 224 us -> 224 us (level)
  no operation moved by 1% of the time
where the time goes in v1:
time: 224 us; the launch traced here: 223 us
  waiting for transfers between devices  80.4 us (36%)
  matrix products  54.9 us (25%)
  blocking collectives  28.5 us (13%)
  local copies, waits for them, and re-layouts  24.8 us (11%)
  other arithmetic  21.3 us (10%)
  between operations  13.2 us (6%)
    unnamed x6, waiting for transfers between devices  32.7 us
    reduce_scatter x1, waiting for transfers between devices, shards(): lax.psum_scatter(jnp.dot(attended, out_weight, preferred_element_type=jnp...  27.3 us
    dot_general x1, matrix products, shards(): jnp.einsum('qhd,khd->hqk', shaped, key_heads, preferred_element_type=jnp....  22.6 us
    dot_general x1, matrix products, shards(): jnp.einsum('hqk,khd->qhd', softened.astype(jnp.bfloat16), value_heads, pr...  22 us
    unnamed x8, local copies, waits for them, and re-layouts  21.9 us
    reduce_sum x1, other arithmetic, shards(): normal_sum = jnp.sum(softened, axis=-1)  21.1 us
    all_gather x1, waiting for transfers between devices, shards(): all_queries = lax.all_gather(query_block, 'ctx', axis=0, tiled=True)  20.3 us
    pmax x1, blocking collectives, shards(): highest = lax.pmax(running, 'ctx')  16.9 us
  transfers between devices with their start and end apart: 4, of which 3 were waited for; matrix products, arithmetic and copies ran while one was open for 19% of the time, Pallas kernels for 0%

profile of v1, /device:TPU:0, one launch (start us, length us, event | category | flops | bytes accessed | tf_op | source)
XLA Modules:
  0.0 223.2 jit_solution(15220883077394763500)
XLA Ops:
  6.5 1.1 slice_bitcast_fusion.3
  7.6 0.1 pad_maximum_fusion
  7.7 11.6 %all_to_all.5 = bf16[4,32,1536]{2,1,0:T(8,128)(2,1)} all-to-all(bf16[4,32,1536]{2,1,0:T(8,128)(2,1)S(1)} %pad_maximum_fusion), channel_id=1, replica_groups=mesh['abl'=2,'head'=4,'ctx'=4] {'head'}, dimensions={0} | all-to-all | bytes 786432 | tf_op jit(solution)/shard_map/all_to_all | solution.py:19
  19.3 0.0 reduce-scatter.12.cloned.1.call-start
  19.3 8.8 %copy.19 = bf16[2048,1536]{0,1:T(8,128)(2,1)} copy(bf16[2048,1536]{1,0:T(8,128)(2,1)} %param.6) | data formatting | bytes 12582912 | tf_op args[1]
  28.1 8.8 %copy.22 = bf16[2048,1536]{0,1:T(8,128)(2,1)} copy(bf16[2048,1536]{1,0:T(8,128)(2,1)} %param.7) | data formatting | bytes 12582912 | tf_op args[2]
  36.8 0.1 broadcast_bitcast_fusion
  36.9 20.3 %all-gather.2.cloned.1.call-done = bf16[512,1536]{1,0:T(8,128)(2,1)} async-done(((bf16[128,1536]{1,0:T(8,128)(2,1)}), bf16[512,1536]{1,0:T(8,128)(2,1)}) %all-gather.2.cloned.1.call-update) | async-done | bytes 1572880 | tf_op jit(solution)/shard_map/all_gather | solution.py:27
  57.2 1.7 copy.18
  59.0 22.6 %fusion = (f32[12,512]{1,0:T(8,128)S(1)}, f32[12,512,2048]{2,1,0:T(8,128)}) fusion(pred[2048]{0:T(1024)(128)(4,1)S(1)} %broadcast_bitcast_fusion, bf16[512,12,128]{0,2,1:T(8,128)(2,1)S(1)} %bitcast.40, bf16[2048,12,128]{0,2,1:T(8,128)(2,1)} %bitcast.39), kind=kOutput, calls=%fused_computation.2 | convolution fusion | flops 3258968064 | bytes 58222592 | tf_op jit(solution)/shard_map/qhd,khd->hqk/dot_general | solution.py:35
  81.5 16.9 %pmax.7 = f32[12,512]{1,0:T(8,128)S(1)} all-reduce(f32[12,512]{1,0:T(8,128)S(1)} %broadcast_maximum_fusion), channel_id=1, replica_groups=mesh['abl'=2,'head'=4,'ctx'=4] {'ctx'}, use_global_device_ids=true, to_apply=%region_1.2 | all-reduce | flops 6144 | bytes 49152 | tf_op jit(solution)/shard_map/pmax | solution.py:51
  98.5 21.1 %fusion.1 = f32[12,512]{1,0:T(8,128)S(1)} fusion(f32[12,512,2048]{2,1,0:T(8,128)} %get-tuple-element.13, f32[12,512]{1,0:T(8,128)S(1)} %broadcast_maximum_fusion, pred[2048]{0:T(1024)(128)(4,1)S(1)} %broadcast_bitcast_fusion), kind=kLoop, calls=%fused_computation.3 | loop fusion | flops 50325504 | bytes 50382848 | tf_op jit(solution)/shard_map/reduce_sum | solution.py:42
  119.6 0.8 copy.27
  120.4 0.0 reduce-scatter.10.cloned.1.call-start
  120.5 22.0 %fusion.7 = bf16[512,12,128]{0,2,1:T(8,128)(2,1)S(1)} fusion(bf16[2048,12,128]{0,2,1:T(8,128)(2,1)} %bitcast.41, f32[12,512,2048]{2,1,0:T(8,128)} %get-tuple-element.13, f32[12,512]{1,0:T(8,128)S(1)} %broadcast_maximum_fusion, pred[2048]{0:T(1024)(128)(4,1)S(1)} %broadcast_bitcast_fusion, f32[512,12]{0,1:T(8,128)S(1)} %get-tuple-element.10, ...), kind=kOutput, calls=%fused_computation.10 | convolution fusion | flops 3273916416 | bytes 58271744 | tf_op jit(solution)/shard_map/hqk,khd->qhd/dot_general | solution.py:43
  142.5 1.6 copy.25
  144.1 0.2 reduce-scatter.8.cloned.1.call-start
  144.3 0.0 reduce-scatter.12.cloned.1.call-done
  144.4 0.8 copy.28
  145.2 32.7 %reduce-scatter.10.cloned.1.call-done = bf16[128,1536]{1,0:T(8,128)(2,1)} async-done(((bf16[512,1536]{1,0:T(8,128)(2,1)}), bf16[128,1536]{1,0:T(8,128)(2,1)}) %reduce-scatter.10.cloned.1.call-update) | async-done | bytes 393232
  177.8 1.2 copy.26
  179.1 0.1 fusion.10
  179.2 10.2 %convolution_convert_fusion = bf16[128,6144]{1,0:T(8,128)(2,1)} fusion(bf16[128,1536]{0,1:T(8,128)(2,1)S(1)} %fusion.10, bf16[1536,6144]{1,0:T(8,128)(2,1)} %param.9), kind=kOutput, calls=%fused_computation.7 | convolution fusion | flops 2416705536 | bytes 20840448 | tf_op jit(solution)/shard_map/dot_general | solution.py:65
  189.4 27.3 %reduce-scatter.8.cloned.1.call-done = bf16[32,6144]{1,0:T(8,128)(2,1)} async-done(((bf16[128,6144]{1,0:T(8,128)(2,1)}), bf16[32,6144]{1,0:T(8,128)(2,1)}) %reduce-scatter.8.cloned.1.call-update) | async-done | bytes 393232 | tf_op jit(solution)/shard_map/reduce_scatter | solution.py:64
  (11 shorter events, 0.1 us)
Async XLA Ops:
  6.5 30.3 %copy-start = (s32[16]{0:T(128)S(1)}, s32[16]{0:T(128)}, u32[]{:S(2)}) copy-start(s32[16]{0:T(128)} %param.8) | copy-start | bytes 196
  6.5 50.7 %all-gather.2.cloned.1.call-start = ((), (), s32[]{:S(2)}) async-start(), calls=%async_computation.4 | async-start | bytes 1966080 | tf_op jit(solution)/shard_map/all_gather | solution.py:27
  19.3 125.1 %reduce-scatter.12.cloned.1.call-start = ((), (), s32[]{:S(2)}) async-start(), calls=%async_computation.7 | async-start | bytes 163840
  120.4 57.4 %reduce-scatter.10.cloned.1.call-start = ((), (), s32[]{:S(2)}) async-start(), calls=%async_computation.6 | async-start | bytes 1966080
  144.1 72.6 %reduce-scatter.8.cloned.1.call-start = ((), (), s32[]{:S(2)}) async-start(), calls=%async_computation.5 | async-start | bytes 1966080 | tf_op jit(solution)/shard_map/reduce_scatter | solution.py:64
Sparse Core Ops, SparseCore 0:
  19.4 37.8 all-gather.1
  120.5 17.4 reduce-scatter.11
  144.2 33.5 reduce-scatter.9
  189.5 27.1 reduce-scatter.7
